TPU v7x, 32 devices: a whole 2x2x4 slice. The times are simulated.
32 devices in a mesh: groups: 2 (over x), ctx: 16 (over z, y, core).
Axes of the slice: x: 2, y: 2, z: 4, core: 2. Of those that a mesh axis runs over, the one named last changes fastest.
Arguments:
- queries: bfloat16 [8192, 2560], P(('groups', 'ctx')), parts along dimension 0, may hold values from -6 to 6
- keys: bfloat16 [8192, 2560], P(('groups', 'ctx')), parts along dimension 0, may hold values from -6 to 6
- values: bfloat16 [8192, 2560], P(('groups', 'ctx')), parts along dimension 0, may hold values from -6 to 6
- kv_lists: int32 [16, 4, 2, 8], P('ctx'), may hold values from 0 to 7, as said below
- kv_counts: int32 [16, 4, 2], P('ctx'), may hold values from 0 to 8, as said below
Outputs:
- attended: bfloat16 [8192, 2560], P(('groups', 'ctx')), parts along dimension 0
There are 2 independent parts, one for each index of `groups`. A program takes and returns all parts, laid end to end along the dimension named above; an argument that names none is the same for every part. Nothing has to cross between parts.
Inputs may be any that keep to these rules, and one draw needn't show every extreme that they name: For every device d, level k and side s, the first 8 // 2**k entries of kv_lists[d, k, s] are distinct block indices; later entries are never read. kv_counts[d, k, s] is at most 8 // 2**k and reaches it for some device at every level and side; it is 0 exactly where the partner d - 2**k (s = 0) or d + 2**k (s = 1) lies outside 0 to 15, else 1 or more.
All inputs are finite; a program needn't handle non-finite values.
Results may differ from a plain program's by a relative error of at most 0.005.
Values may be sent and summed in bfloat16 or wider, within the bound.
A program may use at most 128 MiB of HBM per device.

v0:
```python
import math
import jax
import jax.numpy as jnp
from jax import lax
from jax.sharding import PartitionSpec as P

HEAD = 128
masked_score = -1e30


def from_behind(block, axis, distance):
    devices = range(lax.axis_size(axis))
    route = [(i - distance, i) for i in devices if i - distance in devices]
    return lax.ppermute(block, axis, route)


def attend(carried, query_heads, key_rows, value_rows, allowed):
    best_score, weight_total, weighted = carried
    head_count = query_heads.shape[1]
    head_size = query_heads.shape[2]
    key_heads = key_rows.reshape(key_rows.shape[0], head_count, head_size)
    value_heads = value_rows.reshape(value_rows.shape[0], head_count, head_size)
    scores = jnp.einsum(
        "qhd,khd->hqk", query_heads, key_heads, preferred_element_type=jnp.float32
    ) * (1.0 / math.sqrt(head_size))
    if allowed is not None:
        scores = jnp.where(allowed[None, None, :], scores, masked_score)
    fresh_best = jnp.maximum(best_score, jnp.max(scores, axis=-1))
    weights = jnp.exp(scores - fresh_best[:, :, None])
    factor = jnp.exp(best_score - fresh_best)
    weight_total = weight_total * factor + jnp.sum(weights, axis=-1)
    mixed_values = jnp.einsum(
        "hqk,khd->qhd",
        weights.astype(jnp.bfloat16),
        value_heads,
        preferred_element_type=jnp.float32,
    )
    weighted = weighted * jnp.transpose(factor)[:, :, None] + mixed_values
    return (fresh_best, weight_total, weighted)


def shards(queries, keys, values, kv_lists, kv_counts):
    row_count = queries.shape[0]
    width = queries.shape[1]
    head_count = width // HEAD
    block_count = kv_lists.shape[3]
    level_count = kv_lists.shape[1]
    block_rows = row_count // block_count
    query_heads = queries.reshape(row_count, head_count, HEAD)
    carried = (
        jnp.full((head_count, row_count), masked_score, jnp.float32),
        jnp.zeros((head_count, row_count), jnp.float32),
        jnp.zeros((row_count, head_count, HEAD), jnp.float32),
    )
    carried = attend(carried, query_heads, keys, values, None)
    key_blocks = keys.reshape(block_count, block_rows, width)
    value_blocks = values.reshape(block_count, block_rows, width)
    every_list = lax.all_gather(kv_lists, "ctx", axis=0, tiled=True)
    here_index = lax.axis_index("ctx")
    ctx_count = lax.axis_size("ctx")
    for level_id in range(level_count):
        distance = 1 << level_id
        capacity = block_count >> level_id
        for side_id in range(2):
            offset = distance if side_id == 0 else -distance
            counted = kv_counts[0, level_id, side_id]
            allowed = jnp.arange(capacity * block_rows, dtype=jnp.int32) // block_rows < counted
            target = jnp.clip(here_index + offset, 0, ctx_count - 1)
            wanted = lax.dynamic_index_in_dim(every_list, target, 0, keepdims=False)[
                level_id, side_id, :capacity
            ]
            packed = jnp.stack(
                [jnp.take(key_blocks, wanted, axis=0), jnp.take(value_blocks, wanted, axis=0)]
            )
            arrived = from_behind(packed, "ctx", offset)
            far_keys = arrived[0]
            far_values = arrived[1]
            carried = attend(
                carried,
                query_heads,
                far_keys.reshape(capacity * block_rows, width),
                far_values.reshape(capacity * block_rows, width),
                allowed,
            )
    best_score, weight_total, weighted = carried
    result = weighted / jnp.transpose(weight_total)[:, :, None]
    return result.reshape(row_count, width).astype(jnp.bfloat16)


def solution(mesh):
    in_specs = (
        P(("groups", "ctx"), None),
        P(("groups", "ctx"), None),
        P(("groups", "ctx"), None),
        P("ctx", None, None, None),
        P("ctx", None, None),
    )
    out_specs = P(("groups", "ctx"), None)
    return jax.shard_map(shards, mesh=mesh, in_specs=in_specs, out_specs=out_specs, check_vma=False)
```

profile of v0, /device:TPU:10, one launch (start us, length us, event | category | flops | bytes accessed | tf_op | source)
XLA Modules:
  0.0 219.9 jit_solution(879587065999367864)
XLA Ops:
  0.8 19.0 %all_gather.3 = s32[16,4,2,8]{3,1,2,0:T(4,128)S(1)} all-gather(s32[1,4,2,8]{3,1,2,0:T(4,128)S(1)} %copy.64), channel_id=1, replica_groups=mesh['groups'=2,'ctx'=16] {'ctx'}, dimensions={0}, use_global_device_ids=true | all-gather | bytes 4352 | tf_op jit(solution)/shard_map/all_gather | solution.py:58
  26.8 2.4 %collective-permute-start.1 = (bf16[2,8,32,2560]{3,2,1,0:T(8,128)(2,1)}, bf16[2,8,32,2560]{3,2,1,0:T(8,128)(2,1)}, u32[]{:S(2)}, u32[]{:S(2)}) collective-permute-start(bf16[2,8,32,2560]{3,2,1,0:T(8,128)(2,1)} %pad_maximum_fusion.1), channel_id=1, source_target_pairs={{1,0},{2,1},{3,2},{4,3},{5,4},{6,5},{7,6},{8,7},{9,8},{10,9},{11,1... | collective-permute-start | bytes 7864328 | tf_op jit(solution)/shard_map/ppermute | solution.py:14
  42.9 6.1 %collective-permute-start.3 = (bf16[2,4,32,2560]{3,2,1,0:T(8,128)(2,1)}, bf16[2,4,32,2560]{3,2,1,0:T(8,128)(2,1)}, u32[]{:S(2)}, u32[]{:S(2)}) collective-permute-start(bf16[2,4,32,2560]{3,2,1,0:T(8,128)(2,1)} %pad_maximum_fusion.3), channel_id=1, source_target_pairs={{2,0},{3,1},{4,2},{5,3},{6,4},{7,5},{8,6},{9,7},{10,8},{11,9},{12,... | collective-permute-start | bytes 3932168 | tf_op jit(solution)/shard_map/ppermute | solution.py:14
  79.9 3.2 %multiply_reduce_fusion = (f32[20,256]{1,0:T(8,128)S(1)}, f32[20,256,256]{1,2,0:T(8,128)}) fusion(bf16[256,20,128]{0,2,1:T(8,128)(2,1)S(1)} %bitcast.392, bf16[256,20,128]{0,2,1:T(8,128)(2,1)S(1)} %bitcast.417), kind=kOutput, calls=%fused_computation.21 | convolution fusion | flops 338160640 | bytes 7884800 | tf_op jit(solution)/shard_map/qhd,khd->hqk/dot_general | solution.py:23
  83.2 11.3 %collective-permute-done.7 = bf16[2,1,32,2560]{3,2,1,0:T(8,128)(2,1)} collective-permute-done((bf16[2,1,32,2560]{3,2,1,0:T(8,128)(2,1)}, bf16[2,1,32,2560]{3,2,1,0:T(8,128)(2,1)}, u32[]{:S(2)}, u32[]{:S(2)}) %collective-permute-start.7) | collective-permute-done | bytes 327712 | tf_op jit(solution)/shard_map/ppermute | solution.py:14
  96.9 3.5 %collective-permute-done.6 = bf16[2,1,32,2560]{3,2,1,0:T(8,128)(2,1)S(1)} collective-permute-done((bf16[2,1,32,2560]{3,2,1,0:T(8,128)(2,1)S(1)}, bf16[2,1,32,2560]{3,2,1,0:T(8,128)(2,1)S(1)}, u32[]{:S(2)}, u32[]{:S(2)}) %collective-permute-start.6) | collective-permute-done | bytes 327712 | tf_op jit(solution)/shard_map/ppermute | solution.py:14
  100.5 9.0 %collective-permute-start.5 = (bf16[2,2,32,2560]{3,2,1,0:T(8,128)(2,1)}, bf16[2,2,32,2560]{3,2,1,0:T(8,128)(2,1)}, u32[]{:S(2)}, u32[]{:S(2)}) collective-permute-start(bf16[2,2,32,2560]{3,2,1,0:T(8,128)(2,1)} %pad_maximum_fusion.5), channel_id=1, source_target_pairs={{4,0},{5,1},{6,2},{7,3},{8,4},{9,5},{10,6},{11,7},{12,8},{13,9},{1... | collective-permute-start | bytes 1966088 | tf_op jit(solution)/shard_map/ppermute | solution.py:14
  113.4 6.9 %collective-permute-done.5 = bf16[2,2,32,2560]{3,2,1,0:T(8,128)(2,1)} collective-permute-done((bf16[2,2,32,2560]{3,2,1,0:T(8,128)(2,1)}, bf16[2,2,32,2560]{3,2,1,0:T(8,128)(2,1)}, u32[]{:S(2)}, u32[]{:S(2)}) %collective-permute-start.5) | collective-permute-done | bytes 655392 | tf_op jit(solution)/shard_map/ppermute | solution.py:14
  120.3 3.9 %collective-permute-start.4 = (bf16[2,2,32,2560]{3,2,1,0:T(8,128)(2,1)}, bf16[2,2,32,2560]{3,2,1,0:T(8,128)(2,1)}, u32[]{:S(2)}, u32[]{:S(2)}) collective-permute-start(bf16[2,2,32,2560]{3,2,1,0:T(8,128)(2,1)} %pad_maximum_fusion.4), channel_id=1, source_target_pairs={{0,4},{1,5},{2,6},{3,7},{4,8},{5,9},{6,10},{7,11},{8,12},{9,13},{1... | collective-permute-start | bytes 1966088 | tf_op jit(solution)/shard_map/ppermute | solution.py:14
  126.3 6.8 %collective-permute-done.4 = bf16[2,2,32,2560]{3,2,1,0:T(8,128)(2,1)} collective-permute-done((bf16[2,2,32,2560]{3,2,1,0:T(8,128)(2,1)}, bf16[2,2,32,2560]{3,2,1,0:T(8,128)(2,1)}, u32[]{:S(2)}, u32[]{:S(2)}) %collective-permute-start.4) | collective-permute-done | bytes 655392 | tf_op jit(solution)/shard_map/ppermute | solution.py:14
  137.0 2.0 fusion.135
  139.1 2.0 fusion.136
  141.1 3.8 %collective-permute-done.3 = bf16[2,4,32,2560]{3,2,1,0:T(8,128)(2,1)} collective-permute-done((bf16[2,4,32,2560]{3,2,1,0:T(8,128)(2,1)}, bf16[2,4,32,2560]{3,2,1,0:T(8,128)(2,1)}, u32[]{:S(2)}, u32[]{:S(2)}) %collective-permute-start.3) | collective-permute-done | bytes 1310752 | tf_op jit(solution)/shard_map/ppermute | solution.py:14
  144.9 2.5 %fusion.127 = (bf16[1,4,32,2560]{3,2,1,0:T(8,128)(2,1)}, bf16[1,4,32,2560]{3,2,1,0:T(8,128)(2,1)}) fusion(bf16[2,4,32,2560]{3,2,1,0:T(8,128)(2,1)} %collective-permute-done.3), kind=kLoop, calls=%fused_computation.273 | loop fusion | bytes 2621440 | tf_op jit(solution)/shard_map/slice | solution.py:77
  147.4 2.3 %reshape_reshape_squeeze.54 = bf16[128,20,128]{2,1,0:T(8,128)(2,1)} reshape(bf16[1,4,32,2560]{3,2,1,0:T(8,128)(2,1)} %get-tuple-element.57) | data formatting | bytes 1310720 | tf_op jit(solution)/shard_map/reshape;reshape;squeeze | solution.py:21
  149.7 2.5 %fusion.126 = (bf16[1,4,32,2560]{3,2,1,0:T(8,128)(2,1)}, bf16[1,4,32,2560]{3,2,1,0:T(8,128)(2,1)}) fusion(bf16[2,4,32,2560]{3,2,1,0:T(8,128)(2,1)} %collective-permute-done.2), kind=kLoop, calls=%fused_computation.272 | loop fusion | bytes 2621440 | tf_op jit(solution)/shard_map/slice | solution.py:77
  152.1 2.2 %reshape_reshape_squeeze.52 = bf16[128,20,128]{2,1,0:T(8,128)(2,1)} reshape(bf16[1,4,32,2560]{3,2,1,0:T(8,128)(2,1)} %get-tuple-element.55) | data formatting | bytes 1310720 | tf_op jit(solution)/shard_map/reshape;reshape;squeeze | solution.py:21
  154.4 2.2 %reshape_reshape_squeeze.53 = bf16[128,20,128]{2,1,0:T(8,128)(2,1)} reshape(bf16[1,4,32,2560]{3,2,1,0:T(8,128)(2,1)} %get-tuple-element.54) | data formatting | bytes 1310720 | tf_op jit(solution)/shard_map/reshape;reshape;squeeze | solution.py:22
  156.6 2.2 %reshape_reshape_squeeze.55 = bf16[128,20,128]{2,1,0:T(8,128)(2,1)} reshape(bf16[1,4,32,2560]{3,2,1,0:T(8,128)(2,1)} %get-tuple-element.56) | data formatting | bytes 1310720 | tf_op jit(solution)/shard_map/reshape;reshape;squeeze | solution.py:22
  158.8 3.9 %bitcast_reduce_fusion.2 = (f32[20,256]{1,0:T(8,128)}, f32[20,128,256]{2,1,0:T(8,128)}) fusion(pred[128]{0:T(512)(128)(4,1)S(1)} %get-tuple-element.131, bf16[256,20,128]{0,2,1:T(8,128)(2,1)S(1)} %bitcast.397, bf16[128,20,128]{2,1,0:T(8,128)(2,1)} %reshape_reshape_squeeze.54), kind=kOutput, calls=%fused_computation.45 | convolution fusion | flops 169733120 | bytes 4608128 | tf_op jit(solution)/shard_map/qhd,khd->hqk/dot_general | solution.py:23
  162.7 2.1 bitcast_reduce_fusion.3
  164.8 3.5 %fusion.125 = (bf16[1,8,32,2560]{3,2,1,0:T(8,128)(2,1)}, bf16[1,8,32,2560]{3,2,1,0:T(8,128)(2,1)}) fusion(bf16[2,8,32,2560]{3,2,1,0:T(8,128)(2,1)} %collective-permute-done.1), kind=kLoop, calls=%fused_computation.271 | loop fusion | bytes 5242880 | tf_op jit(solution)/shard_map/slice | solution.py:77
  168.3 3.5 %reshape_reshape_squeeze.50 = bf16[256,20,128]{2,1,0:T(8,128)(2,1)} reshape(bf16[1,8,32,2560]{3,2,1,0:T(8,128)(2,1)} %get-tuple-element.53) | data formatting | bytes 2621440 | tf_op jit(solution)/shard_map/reshape;reshape;squeeze | solution.py:21
  171.8 3.5 %fusion.124 = (bf16[1,8,32,2560]{3,2,1,0:T(8,128)(2,1)}, bf16[1,8,32,2560]{3,2,1,0:T(8,128)(2,1)}) fusion(bf16[2,8,32,2560]{3,2,1,0:T(8,128)(2,1)} %collective-permute-done), kind=kLoop, calls=%fused_computation.270 | loop fusion | bytes 5242880 | tf_op jit(solution)/shard_map/slice | solution.py:77
  175.3 3.5 %reshape_reshape_squeeze.48 = bf16[256,20,128]{2,1,0:T(8,128)(2,1)} reshape(bf16[1,8,32,2560]{3,2,1,0:T(8,128)(2,1)} %get-tuple-element.51) | data formatting | bytes 2621440 | tf_op jit(solution)/shard_map/reshape;reshape;squeeze | solution.py:21
  178.8 3.5 %reshape_reshape_squeeze.49 = bf16[256,20,128]{2,1,0:T(8,128)(2,1)} reshape(bf16[1,8,32,2560]{3,2,1,0:T(8,128)(2,1)} %get-tuple-element.50) | data formatting | bytes 2621440 | tf_op jit(solution)/shard_map/reshape;reshape;squeeze | solution.py:22
  182.3 5.2 %bitcast_reduce_fusion = (f32[20,256]{1,0:T(8,128)S(1)}, f32[20,256,256]{1,2,0:T(8,128)}) fusion(pred[256]{0:T(512)(128)(4,1)S(1)} %get-tuple-element.125, bf16[256,20,128]{0,2,1:T(8,128)(2,1)S(1)} %bitcast.399, bf16[256,20,128]{2,1,0:T(8,128)(2,1)} %reshape_reshape_squeeze.50), kind=kOutput, calls=%fused_computation.13 | convolution fusion | flops 339471360 | bytes 7885056 | tf_op jit(solution)/shard_map/qhd,khd->hqk/dot_general | solution.py:23
  190.6 2.4 %fusion.4 = f32[20,256]{1,0:T(8,128)} fusion(f32[20,256,256]{1,2,0:T(8,128)S(1)} %get-tuple-element.116, f32[20,256]{1,0:T(8,128)S(1)} %get-tuple-element.37, pred[256]{0:T(512)(128)(4,1)S(1)} %copy-done.48), kind=kLoop, calls=%fused_computation.24 | loop fusion | flops 5237760 | bytes 5284096 | tf_op jit(solution)/shard_map/reduce_sum | solution.py:31
  193.0 3.0 %fusion.10 = f32[20,128,256]{2,1,0:T(8,128)} fusion(f32[20,256,256]{1,2,0:T(8,128)S(1)} %get-tuple-element.116, f32[20,256]{1,0:T(8,128)S(1)} %get-tuple-element.37, pred[256]{0:T(512)(128)(4,1)S(1)} %copy-done.48, bf16[256,20,128]{2,1,0:T(8,128)(2,1)S(1)} %copy-done.8), kind=kOutput, calls=%fused_computation.29 | convolution fusion | flops 340787200 | bytes 9195776 | tf_op jit(solution)/shard_map/hqk,khd->qhd/dot_general | solution.py:32
  197.7 3.7 %fusion.6 = f32[20,256]{1,0:T(8,128)S(1)} fusion(f32[20,256,256]{1,2,0:T(8,128)} %get-tuple-element.114, f32[20,256]{1,0:T(8,128)} %get-tuple-element.36, pred[256]{0:T(512)(128)(4,1)} %copy-done.46), kind=kLoop, calls=%fused_computation.26 | loop fusion | flops 5237760 | bytes 5284096 | tf_op jit(solution)/shard_map/reduce_sum | solution.py:31
  201.4 3.9 %fusion.8 = f32[20,128,256]{2,1,0:T(8,128)S(1)} fusion(f32[20,256,256]{1,2,0:T(8,128)} %get-tuple-element.114, f32[20,256]{1,0:T(8,128)S(1)} %copy-done.38, pred[256]{0:T(512)(128)(4,1)S(1)} %copy-done.47, bf16[256,20,128]{2,1,0:T(8,128)(2,1)S(1)} %copy-done.9), kind=kOutput, calls=%fused_computation.28 | convolution fusion | flops 340787200 | bytes 9195776 | tf_op jit(solution)/shard_map/hqk,khd->qhd/dot_general | solution.py:32
  216.1 2.2 fusion.15
  (199 shorter events, 77.2 us)
Async XLA Ops:
  0.0 21.8 %copy-start.1 = (bf16[256,2560]{1,0:T(8,128)(2,1)S(1)}, bf16[256,2560]{1,0:T(8,128)(2,1)}, u32[]{:S(2)}) copy-start(bf16[256,2560]{1,0:T(8,128)(2,1)} %param.15) | copy-start | bytes 3932164
  25.1 4.1 %copy-start = (bf16[256,2560]{1,0:T(8,128)(2,1)S(1)}, bf16[256,2560]{1,0:T(8,128)(2,1)}, u32[]{:S(2)}) copy-start(bf16[256,2560]{1,0:T(8,128)(2,1)} %param.14) | copy-start | bytes 3932164
  26.8 137.9 %collective-permute-start.1 = (bf16[2,8,32,2560]{3,2,1,0:T(8,128)(2,1)}, bf16[2,8,32,2560]{3,2,1,0:T(8,128)(2,1)}, u32[]{:S(2)}, u32[]{:S(2)}) collective-permute-start(bf16[2,8,32,2560]{3,2,1,0:T(8,128)(2,1)} %pad_maximum_fusion.1), channel_id=1, source_target_pairs={{1,0},{2,1},{3,2},{4,3},{5,4},{6,5},{7,6},{8,7},{9,8},{10,9},{11,1... | collective-permute-start | bytes 7864328 | tf_op jit(solution)/shard_map/ppermute | solution.py:14
  36.5 135.4 %collective-permute-start = (bf16[2,8,32,2560]{3,2,1,0:T(8,128)(2,1)}, bf16[2,8,32,2560]{3,2,1,0:T(8,128)(2,1)}, u32[]{:S(2)}, u32[]{:S(2)}) collective-permute-start(bf16[2,8,32,2560]{3,2,1,0:T(8,128)(2,1)} %pad_maximum_fusion), channel_id=1, source_target_pairs={{0,1},{1,2},{2,3},{3,4},{4,5},{5,6},{6,7},{7,8},{8,9},{9,10},{10,1... | collective-permute-start | bytes 7864328 | tf_op jit(solution)/shard_map/ppermute | solution.py:14
  42.9 102.0 %collective-permute-start.3 = (bf16[2,4,32,2560]{3,2,1,0:T(8,128)(2,1)}, bf16[2,4,32,2560]{3,2,1,0:T(8,128)(2,1)}, u32[]{:S(2)}, u32[]{:S(2)}) collective-permute-start(bf16[2,4,32,2560]{3,2,1,0:T(8,128)(2,1)} %pad_maximum_fusion.3), channel_id=1, source_target_pairs={{2,0},{3,1},{4,2},{5,3},{6,4},{7,5},{8,6},{9,7},{10,8},{11,9},{12,... | collective-permute-start | bytes 3932168 | tf_op jit(solution)/shard_map/ppermute | solution.py:14
  53.5 96.1 %collective-permute-start.2 = (bf16[2,4,32,2560]{3,2,1,0:T(8,128)(2,1)}, bf16[2,4,32,2560]{3,2,1,0:T(8,128)(2,1)}, u32[]{:S(2)}, u32[]{:S(2)}) collective-permute-start(bf16[2,4,32,2560]{3,2,1,0:T(8,128)(2,1)} %pad_maximum_fusion.2), channel_id=1, source_target_pairs={{0,2},{1,3},{2,4},{3,5},{4,6},{5,7},{6,8},{7,9},{8,10},{9,11},{10,... | collective-permute-start | bytes 3932168 | tf_op jit(solution)/shard_map/ppermute | solution.py:14
  62.0 32.5 %collective-permute-start.7 = (bf16[2,1,32,2560]{3,2,1,0:T(8,128)(2,1)}, bf16[2,1,32,2560]{3,2,1,0:T(8,128)(2,1)}, u32[]{:S(2)}, u32[]{:S(2)}) collective-permute-start(bf16[2,1,32,2560]{3,2,1,0:T(8,128)(2,1)} %pad_maximum_fusion.7), channel_id=1, source_target_pairs={{8,0},{9,1},{10,2},{11,3},{12,4},{13,5},{14,6},{15,7},{24,16},{25,... | collective-permute-start | bytes 983048 | tf_op jit(solution)/shard_map/ppermute | solution.py:14
  67.1 2.9 %copy-start.45 = (s32[1,4,2]{1,2,0:T(2,128)S(1)}, s32[1,4,2]{1,2,0:T(2,128)}, u32[]{:S(2)}) copy-start(s32[1,4,2]{1,2,0:T(2,128)} %param.17) | copy-start | bytes 100
  70.0 5.3 %copy-start.19 = (bf16[2,32,2560]{2,1,0:T(8,128)(2,1)S(1)}, bf16[2,32,2560]{2,1,0:T(8,128)(2,1)}, u32[]{:S(2)}) copy-start(bf16[2,32,2560]{2,1,0:T(8,128)(2,1)} %gather_fusion.10) | copy-start | bytes 983044
  70.0 5.3 %copy-start.20 = (bf16[2,32,2560]{2,1,0:T(8,128)(2,1)S(1)}, bf16[2,32,2560]{2,1,0:T(8,128)(2,1)}, u32[]{:S(2)}) copy-start(bf16[2,32,2560]{2,1,0:T(8,128)(2,1)} %gather_fusion.11) | copy-start | bytes 983044
  74.0 108.3 %copy-start.46 = (pred[256]{0:T(512)(128)(4,1)}, pred[256]{0:T(512)(128)(4,1)S(1)}, u32[]{:S(2)}) copy-start(pred[256]{0:T(512)(128)(4,1)S(1)} %get-tuple-element.125) | copy-start | bytes 772
  75.3 4.6 %copy-start.11 = (bf16[256,2560]{0,1:T(8,128)(2,1)S(1)}, bf16[256,2560]{0,1:T(8,128)(2,1)}, u32[]{:S(2)}) copy-start(bf16[256,2560]{0,1:T(8,128)(2,1)} %copy.59) | copy-start | bytes 3932164
  79.9 3.2 %copy-start.22 = (bf16[1,1,32,2560]{3,2,1,0:T(8,128)(2,1)S(1)}, bf16[1,1,32,2560]{3,2,1,0:T(8,128)(2,1)}, u32[]{:S(2)}) copy-start(bf16[1,1,32,2560]{3,2,1,0:T(8,128)(2,1)} %get-tuple-element.61) | copy-start | bytes 491524
  94.5 6.0 %collective-permute-start.6 = (bf16[2,1,32,2560]{3,2,1,0:T(8,128)(2,1)S(1)}, bf16[2,1,32,2560]{3,2,1,0:T(8,128)(2,1)S(1)}, u32[]{:S(2)}, u32[]{:S(2)}) collective-permute-start(bf16[2,1,32,2560]{3,2,1,0:T(8,128)(2,1)S(1)} %pad_maximum_fusion.6), channel_id=1, source_target_pairs={{0,8},{1,9},{2,10},{3,11},{4,12},{5,13},{6,14},{7,15},{16,24},{17,... | collective-permute-start | bytes 983048 | tf_op jit(solution)/shard_map/ppermute | solution.py:14
  100.5 19.8 %collective-permute-start.5 = (bf16[2,2,32,2560]{3,2,1,0:T(8,128)(2,1)}, bf16[2,2,32,2560]{3,2,1,0:T(8,128)(2,1)}, u32[]{:S(2)}, u32[]{:S(2)}) collective-permute-start(bf16[2,2,32,2560]{3,2,1,0:T(8,128)(2,1)} %pad_maximum_fusion.5), channel_id=1, source_target_pairs={{4,0},{5,1},{6,2},{7,3},{8,4},{9,5},{10,6},{11,7},{12,8},{13,9},{1... | collective-permute-start | bytes 1966088 | tf_op jit(solution)/shard_map/ppermute | solution.py:14
  120.3 12.8 %collective-permute-start.4 = (bf16[2,2,32,2560]{3,2,1,0:T(8,128)(2,1)}, bf16[2,2,32,2560]{3,2,1,0:T(8,128)(2,1)}, u32[]{:S(2)}, u32[]{:S(2)}) collective-permute-start(bf16[2,2,32,2560]{3,2,1,0:T(8,128)(2,1)} %pad_maximum_fusion.4), channel_id=1, source_target_pairs={{0,4},{1,5},{2,6},{3,7},{4,8},{5,9},{6,10},{7,11},{8,12},{9,13},{1... | collective-permute-start | bytes 1966088 | tf_op jit(solution)/shard_map/ppermute | solution.py:14
  158.8 3.9 %copy-start.15 = (bf16[128,20,128]{2,1,0:T(8,128)(2,1)S(1)}, bf16[128,20,128]{2,1,0:T(8,128)(2,1)}, u32[]{:S(2)}) copy-start(bf16[128,20,128]{2,1,0:T(8,128)(2,1)} %reshape_reshape_squeeze.52) | copy-start | bytes 1966084
  182.3 5.2 %copy-start.7 = (bf16[256,20,128]{2,1,0:T(8,128)(2,1)S(1)}, bf16[256,20,128]{2,1,0:T(8,128)(2,1)}, u32[]{:S(2)}) copy-start(bf16[256,20,128]{2,1,0:T(8,128)(2,1)} %reshape_reshape_squeeze.48) | copy-start | bytes 3932164
  182.3 5.2 %copy-start.48 = (pred[256]{0:T(512)(128)(4,1)S(1)}, pred[256]{0:T(512)(128)(4,1)}, u32[]{:S(2)}) copy-start(pred[256]{0:T(512)(128)(4,1)} %get-tuple-element.126) | copy-start | bytes 772
  187.5 2.3 %copy-start.25 = (f32[20,256]{1,0:T(8,128)S(1)}, f32[20,256]{1,0:T(8,128)}, u32[]{:S(2)}) copy-start(f32[20,256]{1,0:T(8,128)} %get-tuple-element.101) | copy-start | bytes 61444
  187.5 2.3 %copy-start.27 = (f32[20,256]{1,0:T(8,128)S(1)}, f32[20,256]{1,0:T(8,128)}, u32[]{:S(2)}) copy-start(f32[20,256]{1,0:T(8,128)} %get-tuple-element.103) | copy-start | bytes 61444
  187.5 2.3 %copy-start.29 = (f32[20,256]{1,0:T(8,128)S(1)}, f32[20,256]{1,0:T(8,128)}, u32[]{:S(2)}) copy-start(f32[20,256]{1,0:T(8,128)} %get-tuple-element.105) | copy-start | bytes 61444
  187.5 2.3 %copy-start.31 = (f32[20,256]{1,0:T(8,128)S(1)}, f32[20,256]{1,0:T(8,128)}, u32[]{:S(2)}) copy-start(f32[20,256]{1,0:T(8,128)} %get-tuple-element.107) | copy-start | bytes 61444
  190.6 2.4 %copy-start.8 = (bf16[256,20,128]{2,1,0:T(8,128)(2,1)S(1)}, bf16[256,20,128]{2,1,0:T(8,128)(2,1)}, u32[]{:S(2)}) copy-start(bf16[256,20,128]{2,1,0:T(8,128)(2,1)} %reshape_reshape_squeeze.49) | copy-start | bytes 3932164
  193.0 3.0 %copy-start.10 = (bf16[1,8,32,2560]{3,2,1,0:T(8,128)(2,1)S(1)}, bf16[1,8,32,2560]{3,2,1,0:T(8,128)(2,1)}, u32[]{:S(2)}) copy-start(bf16[1,8,32,2560]{3,2,1,0:T(8,128)(2,1)} %get-tuple-element.52) | copy-start | bytes 3932164
  197.7 3.7 %copy-start.9 = (bf16[256,20,128]{2,1,0:T(8,128)(2,1)S(1)}, bf16[256,20,128]{2,1,0:T(8,128)(2,1)}, u32[]{:S(2)}) copy-start(bf16[256,20,128]{2,1,0:T(8,128)(2,1)} %reshape_reshape_squeeze.51) | copy-start | bytes 3932164
  197.7 3.7 %copy-start.38 = (f32[20,256]{1,0:T(8,128)S(1)}, f32[20,256]{1,0:T(8,128)}, u32[]{:S(2)}) copy-start(f32[20,256]{1,0:T(8,128)} %get-tuple-element.36) | copy-start | bytes 61444
  197.7 3.7 %copy-start.47 = (pred[256]{0:T(512)(128)(4,1)S(1)}, pred[256]{0:T(512)(128)(4,1)}, u32[]{:S(2)}) copy-start(pred[256]{0:T(512)(128)(4,1)} %copy-done.46) | copy-start | bytes 772
  201.4 4.0 %copy-start.3 = (f32[20,128,256]{2,1,0:T(8,128)S(1)}, f32[20,128,256]{2,1,0:T(8,128)}, u32[]{:S(2)}) copy-start(f32[20,128,256]{2,1,0:T(8,128)} %get-tuple-element.112) | copy-start | bytes 7864324
  201.4 4.0 %copy-start.24 = (f32[20,256]{1,0:T(8,128)S(1)}, f32[20,256]{1,0:T(8,128)}, u32[]{:S(2)}) copy-start(f32[20,256]{1,0:T(8,128)} %get-tuple-element.35) | copy-start | bytes 61444
  206.5 3.2 %slice-start = ((s8[5242880]{0:T(1024)(128)(4,1)}), s8[4194304]{0:T(1024)(128)(4,1)S(1)}, s32[]{:S(2)}) async-start(s8[5242880]{0:T(1024)(128)(4,1)} %bitcast.401), calls=%async_computation | async-start | bytes 8388608
  207.4 2.3 %slice-start.1 = ((s8[5242880]{0:T(1024)(128)(4,1)}), s8[1048576]{0:T(1024)(128)(4,1)S(1)}, s32[]{:S(2)}) async-start(s8[5242880]{0:T(1024)(128)(4,1)} %bitcast.401), calls=%async_computation.1 | async-start | bytes 2097152
  (27 other events, 34.6 us)
where the time goes:
time: 221 us; the launch traced here: 220 us
  local copies, waits for them, and re-layouts  67.7 us (31%)
  matrix products  36.2 us (16%)
  waiting for transfers between devices  32.4 us (15%)
  other arithmetic  31.7 us (14%)
  starting transfers between devices  27.9 us (13%)
  blocking collectives  19 us (9%)
  between operations  4.86 us (2%)
    ppermute x8, waiting for transfers between devices, from_behind(): return lax.ppermute(block, axis, route)  32.4 us
    ppermute x8, starting transfers between devices, from_behind(): return lax.ppermute(block, axis, route)  27.9 us
    dot_general x9, matrix products, attend(): jnp.einsum('qhd,khd->hqk', query_heads, key_heads, preferred_element_type...  22.7 us
    all_gather x1, blocking collectives, shards(): every_list = lax.all_gather(kv_lists, 'ctx', axis=0, tiled=True)  19 us
    another operation x16, other arithmetic, shards(): jnp.stack([jnp.take(key_blocks, wanted, axis=0), jnp.take(value_blocks, w...  15.7 us
    slice x8, local copies, waits for them, and re-layouts, shards(): far_values = arrived[1]  15.3 us
    another operation x8, local copies, waits for them, and re-layouts, attend(): key_heads = key_rows.reshape(key_rows.shape[0], head_count, head_size)  13.6 us
    dot_general x9, matrix products, attend(): jnp.einsum('hqk,khd->qhd', weights.astype(jnp.bfloat16), value_heads, pre...  13.5 us
  transfers between devices with their start and end apart: 8, of which 5 were waited for; matrix products, arithmetic and copies ran while one was open for 37% of the time, Pallas kernels for 0%

commit v1 on v0

--- a/solution.py
+++ b/solution.py
@@ -55,7 +55,10 @@
     carried = attend(carried, query_heads, keys, values, None)
     key_blocks = keys.reshape(block_count, block_rows, width)
     value_blocks = values.reshape(block_count, block_rows, width)
-    every_list = lax.all_gather(kv_lists, "ctx", axis=0, tiled=True)
+    size = lax.axis_size("ctx")
+    parts = jnp.stack([kv_lists for _ in range(size)])
+    parts = lax.all_to_all(parts, "ctx", split_axis=0, concat_axis=0)
+    every_list = jnp.concatenate(parts, axis=0)
     here_index = lax.axis_index("ctx")
     ctx_count = lax.axis_size("ctx")
     for level_id in range(level_count):

time: 221 us -> 263 us (1.19)
  waiting for transfers between devices: 32.4 us -> 72.2 us
  blocking collectives: 19 us -> 0 us
  starting transfers between devices: 27.9 us -> 40.6 us
  local copies, waits for them, and re-layouts: 67.7 us -> 78.7 us
  other arithmetic: 31.7 us -> 27.5 us
    ppermute x8, waiting for transfers between devices: 32.4 us -> 72.2 us  [from_behind(): return lax.ppermute(block, axis, route)]
    all_gather x1 -> x0, blocking collectives: 19 us -> none  [shards(): every_list = lax.all_gather(kv_lists, 'ctx', axis=0, tiled=True)]
    gather x6, local copies, waits for them, and re-layouts: 6.68 us -> 16 us  [shards(): jnp.take(key_blocks, wanted, axis=0)]
    ppermute x8, starting transfers between devices: 27.9 us -> 34.3 us  [from_behind(): return lax.ppermute(block, axis, route)]
    all_to_all x0 -> x1, starting transfers between devices: none -> 6.3 us  [shards(): parts = lax.all_to_all(parts, 'ctx', split_axis=0, concat_axis=0)]
    another operation x16 -> x15, other arithmetic: 15.7 us -> 11 us  [shards(): jnp.stack([jnp.take(key_blocks, wanted, axis=0), jnp.take(value_blocks, w...]
    unnamed x106 -> x115, local copies, waits for them, and re-layouts: 8.28 us -> 7.56 us
  transfers between devices with their start and end apart: 8 -> 9, of which waited for: 5 -> 4; matrix products, arithmetic and copies ran while one was open for 37% -> 25% of each run, Pallas kernels for 0% -> 0%
where the time goes in v1:
time: 263 us; the launch traced here: 261 us
  local copies, waits for them, and re-layouts  78.7 us (30%)
  waiting for transfers between devices  72.2 us (27%)
  starting transfers between devices  40.6 us (15%)
  matrix products  37.7 us (14%)
  other arithmetic  27.5 us (10%)
  between operations  4.42 us (2%)
    ppermute x8, waiting for transfers between devices, from_behind(): return lax.ppermute(block, axis, route)  72.2 us
    ppermute x8, starting transfers between devices, from_behind(): return lax.ppermute(block, axis, route)  34.3 us
    dot_general x9, matrix products, attend(): jnp.einsum('qhd,khd->hqk', query_heads, key_heads, preferred_element_type...  24.2 us
    gather x6, local copies, waits for them, and re-layouts, shards(): jnp.take(key_blocks, wanted, axis=0)  16 us
    slice x8, local copies, waits for them, and re-layouts, shards(): far_values = arrived[1]  14.3 us
    another operation x8, local copies, waits for them, and re-layouts, attend(): key_heads = key_rows.reshape(key_rows.shape[0], head_count, head_size)  13.7 us
    dot_general x9, matrix products, attend(): jnp.einsum('hqk,khd->qhd', weights.astype(jnp.bfloat16), value_heads, pre...  13.5 us
    another operation x8, local copies, waits for them, and re-layouts, attend(): value_heads = value_rows.reshape(value_rows.shape[0], head_count, head_size)  12.5 us
  transfers between devices with their start and end apart: 9, of which 4 were waited for; matrix products, arithmetic and copies ran while one was open for 25% of the time, Pallas kernels for 0%

profile of v1, /device:TPU:10, one launch (start us, length us, event | category | flops | bytes accessed | tf_op | source)
XLA Modules:
  0.0 261.1 jit_solution(7687370874658851220)
XLA Ops:
  1.5 6.3 %all-to-all-start = ((s32[16,1,4,2,8]{4,3,2,1,0:T(2,128)}), s32[16,1,4,2,8]{4,3,2,1,0:T(2,128)S(1)}, u32[]{:S(2)}, u32[]{:S(2)}) async-start(s32[16,1,4,2,8]{4,3,2,1,0:T(2,128)} %stack.91), calls=%async_computation | async-start | bytes 131072 | tf_op jit(solution)/shard_map/all_to_all | solution.py:60
  16.7 4.7 %multiply_reduce_fusion = (f32[20,256]{1,0:T(8,128)S(1)}, f32[20,256,256]{1,2,0:T(8,128)}) fusion(bf16[256,20,128]{0,2,1:T(8,128)(2,1)S(1)} %bitcast.387, bf16[256,20,128]{0,2,1:T(8,128)(2,1)} %bitcast.412), kind=kOutput, calls=%fused_computation.21 | convolution fusion | flops 338160640 | bytes 7884800 | tf_op jit(solution)/shard_map/qhd,khd->hqk/dot_general | solution.py:23
  24.6 3.0 %gather_fusion.2 = bf16[8,32,2560]{2,1,0:T(8,128)(2,1)} fusion(bf16[8,32,2560]{2,1,0:T(8,128)(2,1)} %bitcast.405, s32[1024]{0:T(1024)S(1)} %pad_clamp_fusion.4), kind=kCustom, calls=%fused_computation.4.clone | custom fusion | bytes 2621472 | tf_op jit(solution)/shard_map/jit(_take)/gather | solution.py:76
  29.4 3.0 %gather_fusion = bf16[8,32,2560]{2,1,0:T(8,128)(2,1)} fusion(bf16[8,32,2560]{2,1,0:T(8,128)(2,1)} %bitcast.406, s32[1024]{0:T(1024)S(1)} %pad_clamp_fusion.5), kind=kCustom, calls=%fused_computation.clone | custom fusion | bytes 2621472 | tf_op jit(solution)/shard_map/jit(_take)/gather | solution.py:76
  34.2 2.7 %gather_fusion.6 = bf16[4,32,2560]{2,1,0:T(8,128)(2,1)} fusion(bf16[8,32,2560]{2,1,0:T(8,128)(2,1)} %bitcast.407, s32[1024]{0:T(1024)S(1)} %pad_clamp_fusion.2), kind=kCustom, calls=%fused_computation.7.clone | custom fusion | bytes 1310736 | tf_op jit(solution)/shard_map/jit(_take)/gather | solution.py:76
  41.7 2.6 %gather_fusion.10 = bf16[2,32,2560]{2,1,0:T(8,128)(2,1)} fusion(bf16[8,32,2560]{2,1,0:T(8,128)(2,1)} %bitcast.409, s32[1024]{0:T(1024)S(1)} %pad_clamp_fusion), kind=kCustom, calls=%fused_computation.10.clone | custom fusion | bytes 655368 | tf_op jit(solution)/shard_map/jit(_take)/gather | solution.py:76
  45.7 2.6 %gather_fusion.8 = bf16[2,32,2560]{2,1,0:T(8,128)(2,1)} fusion(bf16[8,32,2560]{2,1,0:T(8,128)(2,1)} %bitcast.410, s32[1024]{0:T(1024)S(1)} %pad_clamp_fusion.1), kind=kCustom, calls=%fused_computation.2.clone | custom fusion | bytes 655368 | tf_op jit(solution)/shard_map/jit(_take)/gather | solution.py:76
  58.0 3.2 %collective-permute-start.1 = (bf16[2,8,32,2560]{3,2,1,0:T(8,128)(2,1)}, bf16[2,8,32,2560]{3,2,1,0:T(8,128)(2,1)}, u32[]{:S(2)}, u32[]{:S(2)}) collective-permute-start(bf16[2,8,32,2560]{3,2,1,0:T(8,128)(2,1)} %pad_maximum_fusion.1), channel_id=1, source_target_pairs={{1,0},{2,1},{3,2},{4,3},{5,4},{6,5},{7,6},{8,7},{9,8},{10,9},{11,1... | collective-permute-start | bytes 7864328 | tf_op jit(solution)/shard_map/ppermute | solution.py:14
  66.7 2.7 %collective-permute-start.3 = (bf16[2,4,32,2560]{3,2,1,0:T(8,128)(2,1)}, bf16[2,4,32,2560]{3,2,1,0:T(8,128)(2,1)}, u32[]{:S(2)}, u32[]{:S(2)}) collective-permute-start(bf16[2,4,32,2560]{3,2,1,0:T(8,128)(2,1)} %pad_maximum_fusion.3), channel_id=1, source_target_pairs={{2,0},{3,1},{4,2},{5,3},{6,4},{7,5},{8,6},{9,7},{10,8},{11,9},{12,... | collective-permute-start | bytes 3932168 | tf_op jit(solution)/shard_map/ppermute | solution.py:14
  70.8 3.3 %collective-permute-start.2 = (bf16[2,4,32,2560]{3,2,1,0:T(8,128)(2,1)}, bf16[2,4,32,2560]{3,2,1,0:T(8,128)(2,1)}, u32[]{:S(2)}, u32[]{:S(2)}) collective-permute-start(bf16[2,4,32,2560]{3,2,1,0:T(8,128)(2,1)} %pad_maximum_fusion.2), channel_id=1, source_target_pairs={{0,2},{1,3},{2,4},{3,5},{4,6},{5,7},{6,8},{7,9},{8,10},{9,11},{10,... | collective-permute-start | bytes 3932168 | tf_op jit(solution)/shard_map/ppermute | solution.py:14
  77.9 54.2 %collective-permute-done.7 = bf16[2,1,32,2560]{3,2,1,0:T(8,128)(2,1)S(1)} collective-permute-done((bf16[2,1,32,2560]{3,2,1,0:T(8,128)(2,1)S(1)}, bf16[2,1,32,2560]{3,2,1,0:T(8,128)(2,1)S(1)}, u32[]{:S(2)}, u32[]{:S(2)}) %collective-permute-start.7) | collective-permute-done | bytes 327712 | tf_op jit(solution)/shard_map/ppermute | solution.py:14
  133.5 4.5 %collective-permute-done.6 = bf16[2,1,32,2560]{3,2,1,0:T(8,128)(2,1)S(1)} collective-permute-done((bf16[2,1,32,2560]{3,2,1,0:T(8,128)(2,1)S(1)}, bf16[2,1,32,2560]{3,2,1,0:T(8,128)(2,1)S(1)}, u32[]{:S(2)}, u32[]{:S(2)}) %collective-permute-start.6) | collective-permute-done | bytes 327712 | tf_op jit(solution)/shard_map/ppermute | solution.py:14
  138.0 16.5 %collective-permute-start.5 = (bf16[2,2,32,2560]{3,2,1,0:T(8,128)(2,1)}, bf16[2,2,32,2560]{3,2,1,0:T(8,128)(2,1)}, u32[]{:S(2)}, u32[]{:S(2)}) collective-permute-start(bf16[2,2,32,2560]{3,2,1,0:T(8,128)(2,1)} %pad_maximum_fusion.5), channel_id=1, source_target_pairs={{4,0},{5,1},{6,2},{7,3},{8,4},{9,5},{10,6},{11,7},{12,8},{13,9},{1... | collective-permute-start | bytes 1966088 | tf_op jit(solution)/shard_map/ppermute | solution.py:14
  158.5 6.9 %collective-permute-done.5 = bf16[2,2,32,2560]{3,2,1,0:T(8,128)(2,1)} collective-permute-done((bf16[2,2,32,2560]{3,2,1,0:T(8,128)(2,1)}, bf16[2,2,32,2560]{3,2,1,0:T(8,128)(2,1)}, u32[]{:S(2)}, u32[]{:S(2)}) %collective-permute-start.5) | collective-permute-done | bytes 655392 | tf_op jit(solution)/shard_map/ppermute | solution.py:14
  165.4 3.9 %collective-permute-start.4 = (bf16[2,2,32,2560]{3,2,1,0:T(8,128)(2,1)S(1)}, bf16[2,2,32,2560]{3,2,1,0:T(8,128)(2,1)}, u32[]{:S(2)}, u32[]{:S(2)}) collective-permute-start(bf16[2,2,32,2560]{3,2,1,0:T(8,128)(2,1)S(1)} %pad_maximum_fusion.4), channel_id=1, source_target_pairs={{0,4},{1,5},{2,6},{3,7},{4,8},{5,9},{6,10},{7,11},{8,12},{9,13},{1... | collective-permute-start | bytes 1966088 | tf_op jit(solution)/shard_map/ppermute | solution.py:14
  171.4 6.6 %collective-permute-done.4 = bf16[2,2,32,2560]{3,2,1,0:T(8,128)(2,1)} collective-permute-done((bf16[2,2,32,2560]{3,2,1,0:T(8,128)(2,1)S(1)}, bf16[2,2,32,2560]{3,2,1,0:T(8,128)(2,1)}, u32[]{:S(2)}, u32[]{:S(2)}) %collective-permute-start.4) | collective-permute-done | bytes 655392 | tf_op jit(solution)/shard_map/ppermute | solution.py:14
  186.0 2.5 fusion.127
  188.5 2.3 reshape_reshape_squeeze.54
  190.8 2.5 fusion.126
  193.3 2.2 reshape_reshape_squeeze.52
  197.8 2.2 reshape_reshape_squeeze.55
  200.0 3.9 %bitcast_reduce_fusion.2 = (f32[20,256]{1,0:T(8,128)}, f32[20,128,256]{2,1,0:T(8,128)}) fusion(pred[128]{0:T(512)(128)(4,1)S(1)} %get-tuple-element.131, bf16[256,20,128]{0,2,1:T(8,128)(2,1)S(1)} %bitcast.392, bf16[128,20,128]{2,1,0:T(8,128)(2,1)} %reshape_reshape_squeeze.54), kind=kOutput, calls=%fused_computation.45 | convolution fusion | flops 169733120 | bytes 4608128 | tf_op jit(solution)/shard_map/qhd,khd->hqk/dot_general | solution.py:23
  205.9 3.5 %fusion.125 = (bf16[1,8,32,2560]{3,2,1,0:T(8,128)(2,1)}, bf16[1,8,32,2560]{3,2,1,0:T(8,128)(2,1)}) fusion(bf16[2,8,32,2560]{3,2,1,0:T(8,128)(2,1)} %collective-permute-done.1), kind=kLoop, calls=%fused_computation.263 | loop fusion | bytes 5242880 | tf_op jit(solution)/shard_map/slice | solution.py:80
  209.4 3.5 %reshape_reshape_squeeze.50 = bf16[256,20,128]{2,1,0:T(8,128)(2,1)} reshape(bf16[1,8,32,2560]{3,2,1,0:T(8,128)(2,1)} %get-tuple-element.53) | data formatting | bytes 2621440 | tf_op jit(solution)/shard_map/reshape;reshape;squeeze | solution.py:21
  212.9 3.5 %fusion.124 = (bf16[1,8,32,2560]{3,2,1,0:T(8,128)(2,1)}, bf16[1,8,32,2560]{3,2,1,0:T(8,128)(2,1)}) fusion(bf16[2,8,32,2560]{3,2,1,0:T(8,128)(2,1)} %collective-permute-done), kind=kLoop, calls=%fused_computation.262 | loop fusion | bytes 5242880 | tf_op jit(solution)/shard_map/slice | solution.py:80
  216.5 3.5 %reshape_reshape_squeeze.48 = bf16[256,20,128]{2,1,0:T(8,128)(2,1)} reshape(bf16[1,8,32,2560]{3,2,1,0:T(8,128)(2,1)} %get-tuple-element.51) | data formatting | bytes 2621440 | tf_op jit(solution)/shard_map/reshape;reshape;squeeze | solution.py:21
  220.0 3.5 %reshape_reshape_squeeze.49 = bf16[256,20,128]{2,1,0:T(8,128)(2,1)} reshape(bf16[1,8,32,2560]{3,2,1,0:T(8,128)(2,1)} %get-tuple-element.50) | data formatting | bytes 2621440 | tf_op jit(solution)/shard_map/reshape;reshape;squeeze | solution.py:22
  223.5 5.2 %bitcast_reduce_fusion = (f32[20,256]{1,0:T(8,128)S(1)}, f32[20,256,256]{1,2,0:T(8,128)}) fusion(pred[256]{0:T(512)(128)(4,1)S(1)} %get-tuple-element.125, bf16[256,20,128]{0,2,1:T(8,128)(2,1)S(1)} %bitcast.394, bf16[256,20,128]{2,1,0:T(8,128)(2,1)} %reshape_reshape_squeeze.50), kind=kOutput, calls=%fused_computation.13 | convolution fusion | flops 339471360 | bytes 7885056 | tf_op jit(solution)/shard_map/qhd,khd->hqk/dot_general | solution.py:23
  231.8 2.5 fusion.4
  234.3 3.0 %fusion.10 = f32[20,128,256]{2,1,0:T(8,128)} fusion(f32[20,256,256]{1,2,0:T(8,128)S(1)} %get-tuple-element.116, f32[20,256]{1,0:T(8,128)S(1)} %get-tuple-element.37, pred[256]{0:T(512)(128)(4,1)S(1)} %copy-done.52, bf16[256,20,128]{2,1,0:T(8,128)(2,1)S(1)} %copy-done.8), kind=kOutput, calls=%fused_computation.29 | convolution fusion | flops 340787200 | bytes 9195776 | tf_op jit(solution)/shard_map/hqk,khd->qhd/dot_general | solution.py:32
  238.9 3.7 %fusion.6 = f32[20,256]{1,0:T(8,128)S(1)} fusion(f32[20,256,256]{1,2,0:T(8,128)} %get-tuple-element.114, f32[20,256]{1,0:T(8,128)} %get-tuple-element.36, pred[256]{0:T(512)(128)(4,1)} %copy-done.50), kind=kLoop, calls=%fused_computation.26 | loop fusion | flops 5237760 | bytes 5284096 | tf_op jit(solution)/shard_map/reduce_sum | solution.py:31
  242.6 3.9 %fusion.8 = f32[20,128,256]{2,1,0:T(8,128)S(1)} fusion(f32[20,256,256]{1,2,0:T(8,128)} %get-tuple-element.114, f32[20,256]{1,0:T(8,128)S(1)} %copy-done.43, pred[256]{0:T(512)(128)(4,1)S(1)} %copy-done.51, bf16[256,20,128]{2,1,0:T(8,128)(2,1)S(1)} %copy-done.9), kind=kOutput, calls=%fused_computation.28 | convolution fusion | flops 340787200 | bytes 9195776 | tf_op jit(solution)/shard_map/hqk,khd->qhd/dot_general | solution.py:32
  (202 shorter events, 78.5 us)
Async XLA Ops:
  0.0 10.9 %copy-start.1 = (bf16[256,2560]{1,0:T(8,128)(2,1)S(1)}, bf16[256,2560]{1,0:T(8,128)(2,1)}, u32[]{:S(2)}) copy-start(bf16[256,2560]{1,0:T(8,128)(2,1)} %param.14) | copy-start | bytes 3932164
  1.5 23.1 %all-to-all-start = ((s32[16,1,4,2,8]{4,3,2,1,0:T(2,128)}), s32[16,1,4,2,8]{4,3,2,1,0:T(2,128)S(1)}, u32[]{:S(2)}, u32[]{:S(2)}) async-start(s32[16,1,4,2,8]{4,3,2,1,0:T(2,128)} %stack.91), calls=%async_computation | async-start | bytes 131072 | tf_op jit(solution)/shard_map/all_to_all | solution.py:60
  14.3 209.2 %copy-start.50 = (pred[256]{0:T(512)(128)(4,1)}, pred[256]{0:T(512)(128)(4,1)S(1)}, u32[]{:S(2)}) copy-start(pred[256]{0:T(512)(128)(4,1)S(1)} %get-tuple-element.125) | copy-start | bytes 772
  16.7 6.4 %copy-start = (bf16[256,2560]{1,0:T(8,128)(2,1)S(1)}, bf16[256,2560]{1,0:T(8,128)(2,1)}, u32[]{:S(2)}) copy-start(bf16[256,2560]{1,0:T(8,128)(2,1)} %param.15) | copy-start | bytes 3932164
  56.3 5.0 %copy-start.11 = (bf16[8,32,2560]{2,1,0:T(8,128)(2,1)S(1)}, bf16[8,32,2560]{2,1,0:T(8,128)(2,1)}, u32[]{:S(2)}) copy-start(bf16[8,32,2560]{2,1,0:T(8,128)(2,1)} %gather_fusion) | copy-start | bytes 3932164
  56.3 5.0 %copy-start.12 = (bf16[8,32,2560]{2,1,0:T(8,128)(2,1)S(1)}, bf16[8,32,2560]{2,1,0:T(8,128)(2,1)}, u32[]{:S(2)}) copy-start(bf16[8,32,2560]{2,1,0:T(8,128)(2,1)} %gather_fusion.1) | copy-start | bytes 3932164
  58.0 147.9 %collective-permute-start.1 = (bf16[2,8,32,2560]{3,2,1,0:T(8,128)(2,1)}, bf16[2,8,32,2560]{3,2,1,0:T(8,128)(2,1)}, u32[]{:S(2)}, u32[]{:S(2)}) collective-permute-start(bf16[2,8,32,2560]{3,2,1,0:T(8,128)(2,1)} %pad_maximum_fusion.1), channel_id=1, source_target_pairs={{1,0},{2,1},{3,2},{4,3},{5,4},{6,5},{7,6},{8,7},{9,8},{10,9},{11,1... | collective-permute-start | bytes 7864328 | tf_op jit(solution)/shard_map/ppermute | solution.py:14
  61.5 3.8 %copy-start.18 = (bf16[4,32,2560]{2,1,0:T(8,128)(2,1)S(1)}, bf16[4,32,2560]{2,1,0:T(8,128)(2,1)}, u32[]{:S(2)}) copy-start(bf16[4,32,2560]{2,1,0:T(8,128)(2,1)} %gather_fusion.6) | copy-start | bytes 1966084
  61.6 3.8 %copy-start.19 = (bf16[4,32,2560]{2,1,0:T(8,128)(2,1)S(1)}, bf16[4,32,2560]{2,1,0:T(8,128)(2,1)}, u32[]{:S(2)}) copy-start(bf16[4,32,2560]{2,1,0:T(8,128)(2,1)} %gather_fusion.7) | copy-start | bytes 1966084
  63.4 149.5 %collective-permute-start = (bf16[2,8,32,2560]{3,2,1,0:T(8,128)(2,1)}, bf16[2,8,32,2560]{3,2,1,0:T(8,128)(2,1)}, u32[]{:S(2)}, u32[]{:S(2)}) collective-permute-start(bf16[2,8,32,2560]{3,2,1,0:T(8,128)(2,1)} %pad_maximum_fusion), channel_id=1, source_target_pairs={{0,1},{1,2},{2,3},{3,4},{4,5},{5,6},{6,7},{7,8},{8,9},{9,10},{10,1... | collective-permute-start | bytes 7864328 | tf_op jit(solution)/shard_map/ppermute | solution.py:14
  65.3 4.1 %copy-start.17 = (bf16[4,32,2560]{2,1,0:T(8,128)(2,1)S(1)}, bf16[4,32,2560]{2,1,0:T(8,128)(2,1)}, u32[]{:S(2)}) copy-start(bf16[4,32,2560]{2,1,0:T(8,128)(2,1)} %gather_fusion.5) | copy-start | bytes 1966084
  66.7 119.3 %collective-permute-start.3 = (bf16[2,4,32,2560]{3,2,1,0:T(8,128)(2,1)}, bf16[2,4,32,2560]{3,2,1,0:T(8,128)(2,1)}, u32[]{:S(2)}, u32[]{:S(2)}) collective-permute-start(bf16[2,4,32,2560]{3,2,1,0:T(8,128)(2,1)} %pad_maximum_fusion.3), channel_id=1, source_target_pairs={{2,0},{3,1},{4,2},{5,3},{6,4},{7,5},{8,6},{9,7},{10,8},{11,9},{12,... | collective-permute-start | bytes 3932168 | tf_op jit(solution)/shard_map/ppermute | solution.py:14
  69.6 6.9 %copy-start.25 = (bf16[2,32,2560]{2,1,0:T(8,128)(2,1)S(1)}, bf16[2,32,2560]{2,1,0:T(8,128)(2,1)}, u32[]{:S(2)}) copy-start(bf16[2,32,2560]{2,1,0:T(8,128)(2,1)} %gather_fusion.10) | copy-start | bytes 983044
  69.6 6.9 %copy-start.26 = (bf16[2,32,2560]{2,1,0:T(8,128)(2,1)S(1)}, bf16[2,32,2560]{2,1,0:T(8,128)(2,1)}, u32[]{:S(2)}) copy-start(bf16[2,32,2560]{2,1,0:T(8,128)(2,1)} %gather_fusion.11) | copy-start | bytes 983044
  70.8 6.8 %copy-start.23 = (bf16[2,32,2560]{2,1,0:T(8,128)(2,1)S(1)}, bf16[2,32,2560]{2,1,0:T(8,128)(2,1)}, u32[]{:S(2)}) copy-start(bf16[2,32,2560]{2,1,0:T(8,128)(2,1)} %gather_fusion.8) | copy-start | bytes 983044
  70.8 6.8 %copy-start.24 = (bf16[2,32,2560]{2,1,0:T(8,128)(2,1)S(1)}, bf16[2,32,2560]{2,1,0:T(8,128)(2,1)}, u32[]{:S(2)}) copy-start(bf16[2,32,2560]{2,1,0:T(8,128)(2,1)} %gather_fusion.9) | copy-start | bytes 983044
  70.8 120.0 %collective-permute-start.2 = (bf16[2,4,32,2560]{3,2,1,0:T(8,128)(2,1)}, bf16[2,4,32,2560]{3,2,1,0:T(8,128)(2,1)}, u32[]{:S(2)}, u32[]{:S(2)}) collective-permute-start(bf16[2,4,32,2560]{3,2,1,0:T(8,128)(2,1)} %pad_maximum_fusion.2), channel_id=1, source_target_pairs={{0,2},{1,3},{2,4},{3,5},{4,6},{5,7},{6,8},{7,9},{8,10},{9,11},{10,... | collective-permute-start | bytes 3932168 | tf_op jit(solution)/shard_map/ppermute | solution.py:14
  75.3 56.8 %collective-permute-start.7 = (bf16[2,1,32,2560]{3,2,1,0:T(8,128)(2,1)S(1)}, bf16[2,1,32,2560]{3,2,1,0:T(8,128)(2,1)S(1)}, u32[]{:S(2)}, u32[]{:S(2)}) collective-permute-start(bf16[2,1,32,2560]{3,2,1,0:T(8,128)(2,1)S(1)} %pad_maximum_fusion.7), channel_id=1, source_target_pairs={{8,0},{9,1},{10,2},{11,3},{12,4},{13,5},{14,6},{15,7},{24,16},{25,... | collective-permute-start | bytes 983048 | tf_op jit(solution)/shard_map/ppermute | solution.py:14
  77.7 78.0 %copy-start.53 = (pred[32]{0:T(512)(128)(4,1)S(1)}, pred[32]{0:T(512)(128)(4,1)}, u32[]{:S(2)}) copy-start(pred[32]{0:T(512)(128)(4,1)} %get-tuple-element.127) | copy-start | bytes 100
  132.0 6.0 %collective-permute-start.6 = (bf16[2,1,32,2560]{3,2,1,0:T(8,128)(2,1)S(1)}, bf16[2,1,32,2560]{3,2,1,0:T(8,128)(2,1)S(1)}, u32[]{:S(2)}, u32[]{:S(2)}) collective-permute-start(bf16[2,1,32,2560]{3,2,1,0:T(8,128)(2,1)S(1)} %pad_maximum_fusion.6), channel_id=1, source_target_pairs={{0,8},{1,9},{2,10},{3,11},{4,12},{5,13},{6,14},{7,15},{16,24},{17,... | collective-permute-start | bytes 983048 | tf_op jit(solution)/shard_map/ppermute | solution.py:14
  138.0 27.3 %collective-permute-start.5 = (bf16[2,2,32,2560]{3,2,1,0:T(8,128)(2,1)}, bf16[2,2,32,2560]{3,2,1,0:T(8,128)(2,1)}, u32[]{:S(2)}, u32[]{:S(2)}) collective-permute-start(bf16[2,2,32,2560]{3,2,1,0:T(8,128)(2,1)} %pad_maximum_fusion.5), channel_id=1, source_target_pairs={{4,0},{5,1},{6,2},{7,3},{8,4},{9,5},{10,6},{11,7},{12,8},{13,9},{1... | collective-permute-start | bytes 1966088 | tf_op jit(solution)/shard_map/ppermute | solution.py:14
  165.4 12.6 %collective-permute-start.4 = (bf16[2,2,32,2560]{3,2,1,0:T(8,128)(2,1)S(1)}, bf16[2,2,32,2560]{3,2,1,0:T(8,128)(2,1)}, u32[]{:S(2)}, u32[]{:S(2)}) collective-permute-start(bf16[2,2,32,2560]{3,2,1,0:T(8,128)(2,1)S(1)} %pad_maximum_fusion.4), channel_id=1, source_target_pairs={{0,4},{1,5},{2,6},{3,7},{4,8},{5,9},{6,10},{7,11},{8,12},{9,13},{1... | collective-permute-start | bytes 1966088 | tf_op jit(solution)/shard_map/ppermute | solution.py:14
  200.0 3.9 %copy-start.16 = (bf16[128,20,128]{2,1,0:T(8,128)(2,1)S(1)}, bf16[128,20,128]{2,1,0:T(8,128)(2,1)}, u32[]{:S(2)}) copy-start(bf16[128,20,128]{2,1,0:T(8,128)(2,1)} %reshape_reshape_squeeze.52) | copy-start | bytes 1966084
  223.5 5.2 %copy-start.7 = (bf16[256,20,128]{2,1,0:T(8,128)(2,1)S(1)}, bf16[256,20,128]{2,1,0:T(8,128)(2,1)}, u32[]{:S(2)}) copy-start(bf16[256,20,128]{2,1,0:T(8,128)(2,1)} %reshape_reshape_squeeze.48) | copy-start | bytes 3932164
  223.5 5.2 %copy-start.52 = (pred[256]{0:T(512)(128)(4,1)S(1)}, pred[256]{0:T(512)(128)(4,1)}, u32[]{:S(2)}) copy-start(pred[256]{0:T(512)(128)(4,1)} %get-tuple-element.126) | copy-start | bytes 772
  234.2 3.0 %copy-start.10 = (bf16[1,8,32,2560]{3,2,1,0:T(8,128)(2,1)S(1)}, bf16[1,8,32,2560]{3,2,1,0:T(8,128)(2,1)}, u32[]{:S(2)}) copy-start(bf16[1,8,32,2560]{3,2,1,0:T(8,128)(2,1)} %get-tuple-element.52) | copy-start | bytes 3932164
  238.9 3.7 %copy-start.9 = (bf16[256,20,128]{2,1,0:T(8,128)(2,1)S(1)}, bf16[256,20,128]{2,1,0:T(8,128)(2,1)}, u32[]{:S(2)}) copy-start(bf16[256,20,128]{2,1,0:T(8,128)(2,1)} %reshape_reshape_squeeze.51) | copy-start | bytes 3932164
  238.9 3.7 %copy-start.43 = (f32[20,256]{1,0:T(8,128)S(1)}, f32[20,256]{1,0:T(8,128)}, u32[]{:S(2)}) copy-start(f32[20,256]{1,0:T(8,128)} %get-tuple-element.36) | copy-start | bytes 61444
  238.9 3.7 %copy-start.51 = (pred[256]{0:T(512)(128)(4,1)S(1)}, pred[256]{0:T(512)(128)(4,1)}, u32[]{:S(2)}) copy-start(pred[256]{0:T(512)(128)(4,1)} %copy-done.50) | copy-start | bytes 772
  242.6 4.0 %copy-start.3 = (f32[20,128,256]{2,1,0:T(8,128)S(1)}, f32[20,128,256]{2,1,0:T(8,128)}, u32[]{:S(2)}) copy-start(f32[20,128,256]{2,1,0:T(8,128)} %get-tuple-element.112) | copy-start | bytes 7864324
  242.6 4.0 %copy-start.29 = (f32[20,256]{1,0:T(8,128)S(1)}, f32[20,256]{1,0:T(8,128)}, u32[]{:S(2)}) copy-start(f32[20,256]{1,0:T(8,128)} %get-tuple-element.35) | copy-start | bytes 61444
  247.7 3.2 %slice-start = ((s8[5242880]{0:T(1024)(128)(4,1)}), s8[4194304]{0:T(1024)(128)(4,1)S(1)}, s32[]{:S(2)}) async-start(s8[5242880]{0:T(1024)(128)(4,1)} %bitcast.396), calls=%async_computation.1 | async-start | bytes 8388608
  (33 other events, 48.7 us)
